TPU v7x, 512 devices: a whole 4x8x8 slice. The times are simulated.
512 devices in a mesh: freq: 32 (over z, x_lo, core), tm: 16 (over x_hi, y).
Axes of the slice: x: 4 (x_hi: 2, x_lo: 2; x = x_hi * 2 + x_lo), y: 8, z: 8, core: 2. Of those that a mesh axis runs over, the one named last changes fastest.
Arguments:
- observed: bfloat16 [32, 16, 2, 512, 512], P('freq', 'tm'), may hold values from -6 to 6
- source_beams: bfloat16 [32, 16, 2, 256, 512], P('freq', 'tm'), may hold values from -1.1953125 to 1.1953125
- source_order: int32 [256], replicated, may hold values from 0 to 255, each once
- initial_gains: float32 [32, 2, 32, 512], P('freq'), may hold values from -2 to 2, as said below
- blending: float32 [32, 32], replicated, may hold values from 0 to 1, as said below
Outputs:
- residual: bfloat16 [32, 16, 2, 512, 512], P('freq', 'tm')
- smoothed_gains: float32 [32, 2, 32, 512], P('freq', None, 'tm')
Inputs may be any that keep to these rules, and one draw needn't show every extreme that they name: source_order holds every number of 0 to 255 once. Every row of blending is positive and sums to one. `initial_gains`: every complex gain has a magnitude between 0.5 and 2.
All inputs are finite; a program needn't handle non-finite values.
Results may differ from a plain program's by a relative error of at most 0.0034.
Values sent between devices are 32-bit elements; how exact they have to be, the bound alone decides.
No kernel may reach another device: no remote copies, remote signals or barrier semaphores. Data moves between devices by JAX's collectives and lax.ppermute only.
A program may use at most 64 MiB of HBM per device.

v0:
```python
import jax
import jax.numpy as jnp
from jax import lax
from jax.sharding import PartitionSpec as P

S = 512
K = 32
P_SIZE = 8


def apply_gains(gains, beams):
    real_part = gains[0][:, None, :] * beams[0] - gains[1][:, None, :] * beams[1]
    imag_part = gains[0][:, None, :] * beams[1] + gains[1][:, None, :] * beams[0]
    return jnp.stack([real_part, imag_part]).astype(jnp.bfloat16)


def predict(rounded):
    flat = rounded.reshape(2, rounded.shape[1] * rounded.shape[2], rounded.shape[3])
    joined = flat.reshape(2 * flat.shape[1], flat.shape[2])
    turned = jnp.concatenate([flat[1], -flat[0]], axis=0)
    stacked = jnp.stack([joined, turned])
    return lax.dot_general(
        stacked, joined, (((1,), (0,)), ((), ())), preferred_element_type=jnp.float32
    )


def update(totals, gains):
    denominator = totals[:, 2]
    ratio = jnp.stack([totals[:, 0], totals[:, 1]]) / denominator[None]
    return 0.5 * (ratio + gains)


def local(observed, source_beams, source_order, initial_gains, blending):
    observed_block = observed[0, 0]
    beam_block = source_beams[0, 0]
    start_gains = initial_gains[0]
    highest = lax.Precision.HIGHEST
    beam_float = (
        jnp.take(beam_block, source_order, axis=1).reshape(2, K, P_SIZE, S).astype(jnp.float32)
    )
    seeded = apply_gains(start_gains, beam_float)
    misfit = (observed_block.astype(jnp.float32) - predict(seeded)).astype(jnp.bfloat16)
    seeded_flat = seeded.reshape(2, K * P_SIZE, S)
    owned = K // lax.axis_size("tm")
    stacked = jnp.stack(
        [jnp.stack([seeded_flat[0], -seeded_flat[1]]), jnp.stack([seeded_flat[1], seeded_flat[0]])]
    )
    product = lax.dot_general(
        stacked, misfit, (((1, 3), (0, 2)), ((), ())), preferred_element_type=jnp.float32
    )
    product = product.reshape(2, K, P_SIZE, S)
    pull_real = jnp.sum(beam_float[0] * product[0] + beam_float[1] * product[1], axis=1)
    pull_imag = jnp.sum(beam_float[0] * product[1] - beam_float[1] * product[0], axis=1)
    shaped = seeded_flat.reshape(2, K, P_SIZE, S)
    gram_real = jnp.einsum(
        "kjq,kiq->kji", shaped[0], shaped[0], preferred_element_type=jnp.float32
    ) + jnp.einsum("kjq,kiq->kji", shaped[1], shaped[1], preferred_element_type=jnp.float32)
    gram_imag = jnp.einsum(
        "kjq,kiq->kji", shaped[0], shaped[1], preferred_element_type=jnp.float32
    ) - jnp.einsum("kjq,kiq->kji", shaped[1], shaped[0], preferred_element_type=jnp.float32)
    inner_real = jnp.einsum(
        "kji,kip->kjp", gram_real, beam_float[0], precision=highest
    ) + jnp.einsum("kji,kip->kjp", gram_imag, beam_float[1], precision=highest)
    inner_imag = jnp.einsum(
        "kji,kip->kjp", gram_imag, beam_float[0], precision=highest
    ) - jnp.einsum("kji,kip->kjp", gram_real, beam_float[1], precision=highest)
    denominator = jnp.sum(beam_float[0] * inner_real - beam_float[1] * inner_imag, axis=1)
    pull_real = pull_real + start_gains[0] * denominator
    pull_imag = pull_imag + start_gains[1] * denominator
    local_sums = jnp.stack([pull_real, pull_imag, denominator], axis=1)
    totals = lax.psum(local_sums, "tm")
    damped = update(totals, start_gains)
    mixed = jnp.einsum(
        "fg,gcks->fcks",
        blending,
        lax.all_to_all(damped[None], "freq", split_axis=3, concat_axis=0, tiled=True),
        precision=highest,
    )
    returned = lax.all_to_all(mixed, "freq", split_axis=0, concat_axis=3, tiled=True)
    smooth = returned[0]
    final = apply_gains(smooth, beam_float)
    residual = (observed_block.astype(jnp.float32) - predict(final)).astype(jnp.bfloat16)
    gains_out = lax.dynamic_slice_in_dim(smooth, lax.axis_index("tm") * owned, owned, 1)
    return (residual[None, None], gains_out[None])


def solution(mesh):
    return jax.shard_map(
        local,
        mesh=mesh,
        in_specs=(
            P("freq", "tm", None, None, None),
            P("freq", "tm", None, None, None),
            P(),
            P("freq", None, None, None),
            P(),
        ),
        out_specs=(P("freq", "tm", None, None, None), P("freq", None, "tm", None)),
        check_vma=False,
    )
```

profile of v0, /device:TPU:1, one launch (start us, length us, event | category | flops | bytes accessed | tf_op | source)
XLA Modules:
  0.0 244.0 jit_solution(8187503134172178200)
XLA Ops:
  7.2 0.7 compare_select_fusion
  7.9 0.7 compare_and_fusion
  8.6 1.6 copy.125
  10.4 1.7 gather_fusion
  12.1 1.0 broadcast_select_fusion
  14.0 0.7 fusion.58
  14.7 1.0 slice_bitcast_fusion.3
  16.0 0.7 fusion.60
  17.7 1.8 copy.88
  19.5 1.8 copy.87
  21.2 1.0 copy.89
  22.3 1.9 maximum_bitcast_fusion.2
  24.2 1.1 maximum_bitcast_fusion
  25.3 4.1 %convolution_bitcast_fusion = f32[2,256,512]{2,1,0:T(8,128)} fusion(bf16[1,2,256,512]{3,2,1,0:T(8,128)(2,1)} %get-tuple-element.19, bf16[1,2,256,512]{3,2,1,0:T(8,128)(2,1)} %get-tuple-element.18, bf16[512,512,1]{1,0,2:T(8,128)(2,1)S(1)} %bitcast.168, bf16[1,512,512]{1,2,0:T(8,128)(2,1)} %maximum_bitcast_fusion.2, bf16[1,512,512]{1,2,0:T(8,128)(2,1)} %copy.89, ...), kind=kOutput, calls=%fused_computation.7 | convolution fusion | flops 1076363264 | bytes 4718592 | tf_op jit(solution)/shard_map/dot_general | solution.py:48
  29.4 1.7 fusion.21
  31.4 0.5 fusion.7
  32.0 0.7 pad_maximum_fusion
  32.7 150.6 %all-reduce.2.cloned.1.call-done = f32[32,3,512]{2,0,1:T(8,128)} async-done(((f32[32,3,512]{2,0,1:T(8,128)}), f32[32,3,512]{2,0,1:T(8,128)}) %all-reduce.2.cloned.1.call-update) | async-done | bytes 196624 | tf_op jit(solution)/shard_map/psum | solution.py:71
  183.3 0.9 slice_bitcast_fusion.6
  184.5 0.5 reshape.177
  185.0 28.3 %all_to_all.33 = f32[32,1,1024]{2,1,0:T(1,128)S(1)} all-to-all(f32[32,1,1024]{2,1,0:T(1,128)S(1)} %reshape.177), channel_id=1, replica_groups=mesh['freq'=32,'tm'=16] {'freq'}, dimensions={0} | all-to-all | bytes 262144 | tf_op jit(solution)/shard_map/all_to_all | solution.py:76
  213.3 0.5 broadcast.24
  213.8 0.9 reduce
  215.6 0.6 convolution_bitcast_fusion.1
  216.2 0.5 copy.93
  216.6 0.9 reshape.179
  217.5 4.0 %all-to-all-start.1 = ((f32[32,1,1024]{2,1,0:T(1,128)}), f32[32,1,1024]{2,1,0:T(1,128)S(1)}, u32[]{:S(2)}, u32[]{:S(2)}) async-start(f32[32,1,1024]{2,1,0:T(1,128)} %reshape.179), calls=%async_computation.1 | async-start | bytes 262144 | tf_op jit(solution)/shard_map/all_to_all | solution.py:79
  221.5 9.4 %all-to-all-done.1 = f32[32,1,1024]{2,1,0:T(1,128)S(1)} async-done(((f32[32,1,1024]{2,1,0:T(1,128)}), f32[32,1,1024]{2,1,0:T(1,128)S(1)}, u32[]{:S(2)}, u32[]{:S(2)}) %all-to-all-start.1) | async-done | bytes 131104 | tf_op jit(solution)/shard_map/all_to_all | solution.py:79
  230.9 1.0 reduce.1
  233.4 0.8 copy.100
  234.3 1.2 copy-done.5
  235.4 1.7 fusion.2
  (45 shorter events, 5.1 us)
Async XLA Ops:
  7.2 208.4 %copy-start = (f32[32,32]{1,0:T(8,128)S(1)}, f32[32,32]{1,0:T(8,128)}, u32[]{:S(2)}) copy-start(f32[32,32]{1,0:T(8,128)} %param.9) | copy-start | bytes 12292
  7.2 3.1 %copy-start.1 = (f32[1,2,32,512]{3,2,1,0:T(8,128)S(1)}, f32[1,2,32,512]{3,2,1,0:T(8,128)}, u32[]{:S(2)}) copy-start(f32[1,2,32,512]{3,2,1,0:T(8,128)} %param.8) | copy-start | bytes 393220
  7.2 176.1 %all-reduce.2.cloned.1.call-start = ((), (), s32[]{:S(2)}) async-start(), calls=%async_computation.2 | async-start | bytes 393216 | tf_op jit(solution)/shard_map/psum | solution.py:71
  22.3 1.9 copy-start.2
  22.3 1.9 copy-start.3
  22.3 1.9 copy-start.4
  217.5 13.4 %all-to-all-start.1 = ((f32[32,1,1024]{2,1,0:T(1,128)}), f32[32,1,1024]{2,1,0:T(1,128)S(1)}, u32[]{:S(2)}, u32[]{:S(2)}) async-start(f32[32,1,1024]{2,1,0:T(1,128)} %reshape.179), calls=%async_computation.1 | async-start | bytes 262144 | tf_op jit(solution)/shard_map/all_to_all | solution.py:79
  234.2 1.2 copy-start.5
Sparse Core Ops, SparseCore 0:
  32.8 150.4 all-reduce.1
where the time goes:
time: 244 us
  waiting for transfers between devices  160 us (66%)
  blocking collectives  28.3 us (12%)
  local copies, waits for them, and re-layouts  16.3 us (7%)
  between operations  14.3 us (6%)
  other arithmetic  12.3 us (5%)
  matrix products  8.76 us (4%)
  starting transfers between devices  4 us (2%)
    psum x1, waiting for transfers between devices, local(): totals = lax.psum(local_sums, 'tm')  151 us
    all_to_all x1, blocking collectives, local(): lax.all_to_all(damped[None], 'freq', split_axis=3, concat_axis=0, tiled=T...  28.3 us
    all_to_all x1, waiting for transfers between devices, local(): lax.all_to_all(mixed, 'freq', split_axis=0, concat_axis=3, tiled=True)  9.43 us
  transfers between devices with their start and end apart: 2, of which 2 were waited for; matrix products, arithmetic and copies ran while one was open for 0% of the time, Pallas kernels for 0%

commit v1 on v0

v1 whole, which is shorter than its diff:
```python
import jax
import jax.numpy as jnp
from jax import lax
from jax.experimental import pallas as pl
from jax.experimental.pallas import tpu as pltpu
from jax.sharding import PartitionSpec as P

S = 512
K = 32
P_SIZE = 8
N = K * P_SIZE
HALF = 128
LANES = 128
NT_DIMS = (((1,), (1,)), ((), ()))
NN_DIMS = (((1,), (0,)), ((), ()))
TN_DIMS = (((0,), (0,)), ((), ()))
F32 = jnp.float32
BF16 = jnp.bfloat16


def dot(left, right, dims):
    return lax.dot_general(left, right, dims, preferred_element_type=F32)


def expand(rows):
    return jnp.concatenate(
        [jnp.broadcast_to(rows[k : k + 1], (P_SIZE, rows.shape[1])) for k in range(rows.shape[0])],
        axis=0,
    )


def rotated_pair(real, imag, gains_real, gains_imag):
    return (
        (gains_real * real - gains_imag * imag).astype(BF16),
        (gains_real * imag + gains_imag * real).astype(BF16),
    )


def direction_sums(values):
    return jnp.sum(values.reshape(values.shape[0] // P_SIZE, P_SIZE, values.shape[1]), axis=1)


def terms_kernel(observed, catalogue, order, gains, sums, beams, joined, turned):
    source = lax.broadcasted_iota(jnp.int32, (N, N), 0)
    pick = jnp.where(source == order[...], 1.0, 0.0).astype(BF16)
    for part in range(2):
        beams[part] = dot(pick, catalogue[part], TN_DIMS).astype(BF16)
    for half in range(2):
        rows = pl.ds(half * HALF, HALF)
        ks = pl.ds(half * (K // 2), K // 2)
        seeded_real, seeded_imag = rotated_pair(
            beams[0, rows, :].astype(F32),
            beams[1, rows, :].astype(F32),
            expand(gains[0, ks, :]),
            expand(gains[1, ks, :]),
        )
        base = half * 2 * HALF
        joined[pl.ds(base, HALF), :] = seeded_real
        joined[pl.ds(base + HALF, HALF), :] = seeded_imag
        turned[pl.ds(base, HALF), :] = seeded_imag
        turned[pl.ds(base + HALF, HALF), :] = -seeded_real
    row_dir = lax.broadcasted_iota(jnp.int32, (HALF, HALF), 0) // P_SIZE
    col_dir = lax.broadcasted_iota(jnp.int32, (HALF, HALF), 1) // P_SIZE
    same = row_dir == col_dir
    weights = []
    for half in range(2):
        rows = pl.ds(half * HALF, HALF)
        block = joined[pl.ds(half * 2 * HALF, 2 * HALF), :]
        grid = dot(block, block, NT_DIMS)
        gram_real = jnp.where(same, grid[:HALF, :HALF] + grid[HALF:, HALF:], 0.0)
        gram_imag = jnp.where(same, grid[:HALF, HALF:] - grid[HALF:, :HALF], 0.0)
        gram = jnp.concatenate(
            [
                jnp.concatenate([gram_real, gram_imag], axis=1),
                jnp.concatenate([gram_imag, -gram_real], axis=1),
            ],
            axis=0,
        )
        high = gram.astype(BF16)
        low = (gram - high.astype(F32)).astype(BF16)
        both = jnp.concatenate([beams[0, rows, :], beams[1, rows, :]], axis=0)
        inner = dot(high, both, NN_DIMS) + dot(low, both, NN_DIMS)
        real = beams[0, rows, :].astype(F32)
        imag = beams[1, rows, :].astype(F32)
        weights.append(direction_sums(real * inner[:HALF] - imag * inner[HALF:]))
    weight = jnp.concatenate(weights, axis=0)
    everything = joined[...]
    for chunk in range(2):
        cols = pl.ds(chunk * 256, 256)
        model_real = dot(joined[:, cols], everything, TN_DIMS)
        misfit_real = (observed[0, cols, :].astype(F32) - model_real).astype(BF16)
        model_imag = dot(turned[:, cols], everything, TN_DIMS)
        misfit_minus = (model_imag - observed[1, cols, :].astype(F32)).astype(BF16)
        product = dot(everything, misfit_real, NT_DIMS) + dot(turned[...], misfit_minus, NT_DIMS)
        pulls_real, pulls_imag = [], []
        for half in range(2):
            rows = pl.ds(half * HALF, HALF)
            base = half * 2 * HALF
            real = beams[0, rows, cols].astype(F32)
            imag = beams[1, rows, cols].astype(F32)
            product_real = product[base : base + HALF]
            product_imag = product[base + HALF : base + 2 * HALF]
            pulls_real.append(direction_sums(real * product_real + imag * product_imag))
            pulls_imag.append(direction_sums(real * product_imag - imag * product_real))
        weight_here = weight[:, chunk * 256 : chunk * 256 + 256]
        pull_real = jnp.concatenate(pulls_real, axis=0) + 2.0 * gains[0, :, cols] * weight_here
        pull_imag = jnp.concatenate(pulls_imag, axis=0) + 2.0 * gains[1, :, cols] * weight_here
        for group in range(4):
            for side in range(2):
                piece = group * 4 + chunk * 2 + side
                for part, value in enumerate((pull_real, pull_imag, weight_here)):
                    sums[piece, pl.ds(part * 8, 8), :] = value[
                        group * 8 : group * 8 + 8, side * LANES : (side + 1) * LANES
                    ]


def terms(observed, catalogue, order, gains):
    return pl.pallas_call(
        terms_kernel,
        out_shape=(
            jax.ShapeDtypeStruct((16, 24, LANES), F32),
            jax.ShapeDtypeStruct((2, N, S), BF16),
        ),
        scratch_shapes=[pltpu.VMEM((2 * N, S), BF16), pltpu.VMEM((2 * N, S), BF16)],
        cost_estimate=pl.CostEstimate(flops=2 * 10**9, bytes_accessed=2 * 10**6, transcendentals=0),
        name="terms",
    )(observed, catalogue, order, gains)


def peel_kernel(slot, observed, beams, smooth, residual, gains_out, joined, turned):
    for half in range(2):
        rows = pl.ds(half * HALF, HALF)
        base = half * 2 * HALF
        for block in range(4):
            lanes = pl.ds(block * LANES, LANES)
            gains = [
                jnp.concatenate(
                    [expand(smooth[part * 16 + group * 4 + block]) for group in (2 * half, 2 * half + 1)],
                    axis=0,
                )
                for part in range(2)
            ]
            final_real, final_imag = rotated_pair(
                beams[0, rows, lanes].astype(F32), beams[1, rows, lanes].astype(F32), *gains
            )
            joined[pl.ds(base, HALF), lanes] = final_real
            joined[pl.ds(base + HALF, HALF), lanes] = final_imag
            turned[pl.ds(base, HALF), lanes] = final_imag
            turned[pl.ds(base + HALF, HALF), lanes] = -final_real
    everything = joined[...]
    for chunk in range(2):
        cols = pl.ds(chunk * 256, 256)
        model_real = dot(joined[:, cols], everything, TN_DIMS)
        residual[0, cols, :] = (observed[0, cols, :].astype(F32) - model_real).astype(BF16)
        model_imag = dot(turned[:, cols], everything, TN_DIMS)
        residual[1, cols, :] = (observed[1, cols, :].astype(F32) - model_imag).astype(BF16)
    group = slot[0] // 4
    row = (slot[0] % 4) * 2
    for part in range(2):
        for block in range(4):
            gains_out[part, :, pl.ds(block * LANES, LANES)] = smooth[
                part * 16 + group * 4 + block, pl.ds(row, 2), :
            ]


def peel(slot, observed, beams, smooth):
    vmem = pl.BlockSpec(memory_space=pltpu.VMEM)
    return pl.pallas_call(
        peel_kernel,
        out_shape=(
            jax.ShapeDtypeStruct((2, S, S), BF16),
            jax.ShapeDtypeStruct((2, 2, S), F32),
        ),
        in_specs=[pl.BlockSpec(memory_space=pltpu.SMEM), vmem, vmem, vmem],
        scratch_shapes=[pltpu.VMEM((2 * N, S), BF16), pltpu.VMEM((2 * N, S), BF16)],
        cost_estimate=pl.CostEstimate(flops=10**9, bytes_accessed=3 * 10**6, transcendentals=0),
        name="peel",
    )(slot, observed, beams, smooth)


def local(observed, source_beams, source_order, initial_gains, blending):
    freqs, times = lax.axis_size("freq"), lax.axis_size("tm")
    observed_block = observed[0, 0]
    sums, beams = terms(
        observed_block, source_beams[0, 0], source_order.reshape(1, N), initial_gains[0]
    )
    pieces = lax.all_to_all(sums, "tm", split_axis=0, concat_axis=0, tiled=True)
    totals = jnp.sum(pieces, axis=0).reshape(3, 8, LANES)
    damped = 0.5 * (totals[:2] / totals[2])
    sent = jnp.broadcast_to(damped[None], (freqs // 2, 2, 8, LANES)).reshape(freqs, 8, LANES)
    bands = lax.all_to_all(sent, "freq", split_axis=0, concat_axis=0, tiled=True)
    first = (lax.axis_index("freq") // 2) * 2
    rows = lax.dynamic_slice_in_dim(blending, first, 2, 0)
    mixed = jnp.sum(rows[:, :, None, None] * bands[None], axis=1)
    spread = jnp.broadcast_to(mixed[:, None], (2, times, 8, LANES)).reshape(2 * times, 8, LANES)
    groups = [
        [(pair * 2 + core) * times + time for core in range(2) for time in range(times)]
        for pair in range(freqs // 2)
    ]
    smooth = lax.all_to_all(
        spread, ("freq", "tm"), split_axis=0, concat_axis=0, tiled=True, axis_index_groups=groups
    )
    slot = lax.axis_index("tm").reshape(1)
    residual, gains_out = peel(slot, observed_block, beams, smooth)
    return (residual[None, None], gains_out[None])


def solution(mesh):
    return jax.shard_map(
        local,
        mesh=mesh,
        in_specs=(
            P("freq", "tm", None, None, None),
            P("freq", "tm", None, None, None),
            P(),
            P("freq", None, None, None),
            P(),
        ),
        out_specs=(P("freq", "tm", None, None, None), P("freq", None, "tm", None)),
        check_vma=False,
    )
```

time: 244 us -> 68.5 us (0.28)
  waiting for transfers between devices: 160 us -> 19.5 us
  local copies, waits for them, and re-layouts: 16.3 us -> 2 us
  starting transfers between devices: 4 us -> 18.3 us
  between operations: 14.3 us -> 0.72 us
  other arithmetic: 12.3 us -> 0.16 us
  blocking collectives: 28.3 us -> 19.2 us
  matrix products: 8.76 us -> 0 us
  Pallas kernels: 0 us -> 8.28 us
    psum x1 -> x0, waiting for transfers between devices: 151 us -> none  [local(): totals = lax.psum(local_sums, 'tm')]
    all_to_all x1 -> x2, starting transfers between devices: 3.96 us -> 18.3 us  [the longest x1 12.9 us: local(): lax.all_to_all(sent, 'freq', split_axis=0, concat_axis=0, tiled=True)]
    all_to_all x1 -> x2, waiting for transfers between devices: 9.43 us -> 19.5 us  [the longest x1 10.3 us: local(): lax.all_to_all(spread, ('freq', 'tm'), split_axis=0, concat_axis=0, tiled...]
    all_to_all x1, blocking collectives: 28.3 us -> 19.2 us  [local(): pieces = lax.all_to_all(sums, 'tm', split_axis=0, concat_axis=0, tiled=True)]
    dot_general x11 -> x0, matrix products: 8.76 us -> none  [the longest x1 4.08 us: local(): lax.dot_general(stacked, misfit, (((1, 3), (0, 2)), ((), ())), preferred_...]
    pallas_call x0 -> x2, Pallas kernels: none -> 8.28 us  [the longest x1 5.02 us: terms(): pl.pallas_call(terms_kernel, out_shape=(jax.ShapeDtypeStruct((16, 24, LAN...]
    unnamed x17 -> x4, local copies, waits for them, and re-layouts: 4.86 us -> 0.66 us
    another operation x4 -> x0, other arithmetic: 3.76 us -> none  [the longest x2 1.97 us: predict(): stacked = jnp.stack([joined, turned])]
where the time goes in v1:
time: 68.5 us; the launch traced here: 68.1 us
  waiting for transfers between devices  19.5 us (28%)
  blocking collectives  19.2 us (28%)
  starting transfers between devices  18.3 us (27%)
  Pallas kernels  8.28 us (12%)
  local copies, waits for them, and re-layouts  2 us (3%)
  between operations  0.72 us (1%)
    all_to_all x1, blocking collectives, local(): pieces = lax.all_to_all(sums, 'tm', split_axis=0, concat_axis=0, tiled=True)  19.2 us
    all_to_all x1, starting transfers between devices, local(): lax.all_to_all(sent, 'freq', split_axis=0, concat_axis=0, tiled=True)  12.9 us
    all_to_all x1, waiting for transfers between devices, local(): lax.all_to_all(spread, ('freq', 'tm'), split_axis=0, concat_axis=0, tiled...  10.3 us
    all_to_all x1, waiting for transfers between devices, local(): lax.all_to_all(sent, 'freq', split_axis=0, concat_axis=0, tiled=True)  9.18 us
    all_to_all x1, starting transfers between devices, local(): lax.all_to_all(spread, ('freq', 'tm'), split_axis=0, concat_axis=0, tiled...  5.32 us
    pallas_call x1, Pallas kernels, terms(): pl.pallas_call(terms_kernel, out_shape=(jax.ShapeDtypeStruct((16, 24, LAN...  5.02 us
    pallas_call x1, Pallas kernels, peel(): pl.pallas_call(peel_kernel, out_shape=(jax.ShapeDtypeStruct((2, S, S), BF...  3.26 us
  transfers between devices with their start and end apart: 2, of which 2 were waited for; matrix products, arithmetic and copies ran while one was open for 0% of the time, Pallas kernels for 0%

profile of v1, /device:TPU:1, one launch (start us, length us, event | category | flops | bytes accessed | tf_op | source)
XLA Modules:
  0.0 68.1 jit_solution(37743188781174252)
XLA Ops:
  0.6 0.0 copy-start
  0.6 5.0 %terms.1 = (f32[16,24,128]{2,1,0:T(8,128)}, bf16[2,256,512]{2,1,0:T(8,128)(2,1)}) custom-call(bf16[2,512,512]{2,1,0:T(8,128)(2,1)} %bitcast.15, bf16[2,256,512]{2,1,0:T(8,128)(2,1)} %bitcast.17, s32[1,256]{1,0:T(1,128)} %bitcast.19, f32[2,32,512]{2,1,0:T(8,128)} %bitcast.18), custom_call_target="tpu_custom_call" | custom-call | flops 2000000000 | bytes 2000000 | tf_op jit(solution)/shard_map/terms/pallas_call | solution.py:118
  5.7 19.2 %all_to_all.15 = f32[16,24,128]{2,1,0:T(8,128)S(1)} all-to-all(f32[16,24,128]{2,1,0:T(8,128)} %get-tuple-element.7), channel_id=1, replica_groups=mesh['freq'=32,'tm'=16] {'tm'}, dimensions={0} | all-to-all | bytes 393216 | tf_op jit(solution)/shard_map/all_to_all | solution.py:187
  24.9 0.7 broadcast_in_dim.8
  25.6 12.9 %all-to-all-start.1 = ((f32[32,8,128]{2,1,0:T(8,128)}), f32[32,8,128]{2,1,0:T(8,128)S(1)}, u32[]{:S(2)}, u32[]{:S(2)}) async-start(f32[32,8,128]{2,1,0:T(8,128)} %bitcast.6), calls=%async_computation.1 | async-start | bytes 262144 | tf_op jit(solution)/shard_map/all_to_all | solution.py:191
  38.6 0.0 copy-done
  38.6 9.2 %all-to-all-done.1 = f32[32,8,128]{2,1,0:T(8,128)S(1)} async-done(((f32[32,8,128]{2,1,0:T(8,128)}), f32[32,8,128]{2,1,0:T(8,128)S(1)}, u32[]{:S(2)}, u32[]{:S(2)}) %all-to-all-start.1) | async-done | bytes 131104 | tf_op jit(solution)/shard_map/all_to_all | solution.py:191
  47.8 0.1 multiply_reduce_fusion
  47.9 0.7 broadcast_in_dim.9
  48.6 5.3 %all-to-all-start.2 = ((f32[32,8,128]{2,1,0:T(8,128)}), f32[32,8,128]{2,1,0:T(8,128)S(1)}, u32[]{:S(2)}, u32[]{:S(2)}) async-start(f32[32,8,128]{2,1,0:T(8,128)} %bitcast.7), calls=%async_computation.2 | async-start | bytes 262144 | tf_op jit(solution)/shard_map/all_to_all | solution.py:200
  53.9 10.3 %all-to-all-done.2.smooth = f32[32,8,128]{2,1,0:T(8,128)S(1)} async-done(((f32[32,8,128]{2,1,0:T(8,128)}), f32[32,8,128]{2,1,0:T(8,128)S(1)}, u32[]{:S(2)}, u32[]{:S(2)}) %all-to-all-start.2) | async-done | bytes 131104 | tf_op jit(solution)/shard_map/all_to_all | solution.py:200
  64.2 0.0 copy-start.1
  64.2 0.6 copy-done.1
  64.8 3.3 %peel.1 = (bf16[2,512,512]{2,1,0:T(8,128)(2,1)}, f32[2,2,512]{2,1,0:T(2,128)}) custom-call(s32[1]{0:T(128)} %bitcast.slot, bf16[2,512,512]{2,1,0:T(8,128)(2,1)} %bitcast.16, bf16[2,256,512]{2,1,0:T(8,128)(2,1)} %get-tuple-element.6.beams, f32[32,8,128]{2,1,0:T(8,128)} %copy-done.1), custom_call_target="tpu_custom_call" | custom-call | flops 1000000000 | bytes 3000000 | tf_op jit(solution)/shard_map/peel/pallas_call | solution.py:168
  (4 shorter events, 0.0 us)
Async XLA Ops:
  0.6 38.0 %copy-start = (f32[32,32]{1,0:T(8,128)S(1)}, f32[32,32]{1,0:T(8,128)}, u32[]{:S(2)}) copy-start(f32[32,32]{1,0:T(8,128)} %param.9) | copy-start | bytes 12292
  25.6 22.2 %all-to-all-start.1 = ((f32[32,8,128]{2,1,0:T(8,128)}), f32[32,8,128]{2,1,0:T(8,128)S(1)}, u32[]{:S(2)}, u32[]{:S(2)}) async-start(f32[32,8,128]{2,1,0:T(8,128)} %bitcast.6), calls=%async_computation.1 | async-start | bytes 262144 | tf_op jit(solution)/shard_map/all_to_all | solution.py:191
  48.6 15.6 %all-to-all-start.2 = ((f32[32,8,128]{2,1,0:T(8,128)}), f32[32,8,128]{2,1,0:T(8,128)S(1)}, u32[]{:S(2)}, u32[]{:S(2)}) async-start(f32[32,8,128]{2,1,0:T(8,128)} %bitcast.7), calls=%async_computation.2 | async-start | bytes 262144 | tf_op jit(solution)/shard_map/all_to_all | solution.py:200
  64.2 0.6 copy-start.1

commit v2 on v1

--- a/solution.py
+++ b/solution.py
@@ -40,11 +40,31 @@
     return jnp.sum(values.reshape(values.shape[0] // P_SIZE, P_SIZE, values.shape[1]), axis=1)
 
 
-def terms_kernel(observed, catalogue, order, gains, sums, beams, joined, turned):
+def terms_kernel(
+    observed_hbm, catalogue_hbm, order_hbm, gains_hbm, blending_hbm, sums, beams, rows_out,
+    observed, catalogue, order, gains, blending, joined, turned, arrived,
+):
+    copies = [
+        pltpu.make_async_copy(source, target, arrived.at[at])
+        for at, (source, target) in enumerate(
+            (
+                (order_hbm, order),
+                (catalogue_hbm, catalogue),
+                (gains_hbm, gains),
+                (observed_hbm, observed),
+                (blending_hbm, blending),
+            )
+        )
+    ]
+    for copy in copies:
+        copy.start()
+    copies[0].wait()
+    copies[1].wait()
     source = lax.broadcasted_iota(jnp.int32, (N, N), 0)
     pick = jnp.where(source == order[...], 1.0, 0.0).astype(BF16)
     for part in range(2):
         beams[part] = dot(pick, catalogue[part], TN_DIMS).astype(BF16)
+    copies[2].wait()
     for half in range(2):
         rows = pl.ds(half * HALF, HALF)
         ks = pl.ds(half * (K // 2), K // 2)
@@ -85,6 +105,9 @@
         weights.append(direction_sums(real * inner[:HALF] - imag * inner[HALF:]))
     weight = jnp.concatenate(weights, axis=0)
     everything = joined[...]
+    copies[3].wait()
+    copies[4].wait()
+    rows_out[...] = blending[pl.ds((lax.axis_index("freq") // 2) * 2, 2), :]
     for chunk in range(2):
         cols = pl.ds(chunk * 256, 256)
         model_real = dot(joined[:, cols], everything, TN_DIMS)
@@ -114,20 +137,36 @@
                     ]
 
 
-def terms(observed, catalogue, order, gains):
+def terms(*operands):
+    bands = operands[4].shape[0]
     return pl.pallas_call(
         terms_kernel,
         out_shape=(
             jax.ShapeDtypeStruct((16, 24, LANES), F32),
             jax.ShapeDtypeStruct((2, N, S), BF16),
+            jax.ShapeDtypeStruct((2, bands), F32),
         ),
-        scratch_shapes=[pltpu.VMEM((2 * N, S), BF16), pltpu.VMEM((2 * N, S), BF16)],
+        in_specs=[pl.BlockSpec(memory_space=pltpu.HBM)] * 5,
+        out_specs=(pl.BlockSpec(memory_space=pltpu.VMEM),) * 3,
+        scratch_shapes=[
+            pltpu.VMEM((2, S, S), BF16),
+            pltpu.VMEM((2, N, S), BF16),
+            pltpu.VMEM((1, N), jnp.int32),
+            pltpu.VMEM((2, K, S), F32),
+            pltpu.VMEM((bands, bands), F32),
+            pltpu.VMEM((2 * N, S), BF16),
+            pltpu.VMEM((2 * N, S), BF16),
+            pltpu.SemaphoreType.DMA((5,)),
+        ],
+        compiler_params=pltpu.CompilerParams(vmem_limit_bytes=20 * 2**20),
         cost_estimate=pl.CostEstimate(flops=2 * 10**9, bytes_accessed=2 * 10**6, transcendentals=0),
         name="terms",
-    )(observed, catalogue, order, gains)
-
-
-def peel_kernel(slot, observed, beams, smooth, residual, gains_out, joined, turned):
+    )(*[pltpu.with_memory_space_constraint(operand, pltpu.HBM) for operand in operands])
+
+
+def peel_kernel(
+    observed, beams, smooth, residual_hbm, gains_out, residual, joined, turned, sent
+):
     for half in range(2):
         rows = pl.ds(half * HALF, HALF)
         base = half * 2 * HALF
@@ -148,22 +187,33 @@
             turned[pl.ds(base, HALF), lanes] = final_imag
             turned[pl.ds(base + HALF, HALF), lanes] = -final_real
     everything = joined[...]
+    copies = []
     for chunk in range(2):
         cols = pl.ds(chunk * 256, 256)
-        model_real = dot(joined[:, cols], everything, TN_DIMS)
-        residual[0, cols, :] = (observed[0, cols, :].astype(F32) - model_real).astype(BF16)
-        model_imag = dot(turned[:, cols], everything, TN_DIMS)
-        residual[1, cols, :] = (observed[1, cols, :].astype(F32) - model_imag).astype(BF16)
-    group = slot[0] // 4
-    row = (slot[0] % 4) * 2
+        for part, left in enumerate((joined, turned)):
+            model = dot(left[:, cols], everything, TN_DIMS)
+            residual[part, cols, :] = (observed[part, cols, :].astype(F32) - model).astype(BF16)
+            copies.append(
+                pltpu.make_async_copy(
+                    residual.at[part, cols],
+                    residual_hbm.at[part, cols],
+                    sent.at[2 * chunk + part],
+                )
+            )
+            copies[-1].start()
+    slot = lax.axis_index("tm")
+    group = slot // 4
+    row = (slot % 4) * 2
     for part in range(2):
         for block in range(4):
             gains_out[part, :, pl.ds(block * LANES, LANES)] = smooth[
                 part * 16 + group * 4 + block, pl.ds(row, 2), :
             ]
-
-
-def peel(slot, observed, beams, smooth):
+    for copy in copies:
+        copy.wait()
+
+
+def peel(observed, beams, smooth):
     vmem = pl.BlockSpec(memory_space=pltpu.VMEM)
     return pl.pallas_call(
         peel_kernel,
@@ -171,26 +221,35 @@
             jax.ShapeDtypeStruct((2, S, S), BF16),
             jax.ShapeDtypeStruct((2, 2, S), F32),
         ),
-        in_specs=[pl.BlockSpec(memory_space=pltpu.SMEM), vmem, vmem, vmem],
-        scratch_shapes=[pltpu.VMEM((2 * N, S), BF16), pltpu.VMEM((2 * N, S), BF16)],
+        in_specs=[vmem, vmem, vmem],
+        out_specs=(pl.BlockSpec(memory_space=pltpu.HBM), vmem),
+        scratch_shapes=[
+            pltpu.VMEM((2, S, S), BF16),
+            pltpu.VMEM((2 * N, S), BF16),
+            pltpu.VMEM((2 * N, S), BF16),
+            pltpu.SemaphoreType.DMA((4,)),
+        ],
+        compiler_params=pltpu.CompilerParams(vmem_limit_bytes=20 * 2**20),
         cost_estimate=pl.CostEstimate(flops=10**9, bytes_accessed=3 * 10**6, transcendentals=0),
         name="peel",
-    )(slot, observed, beams, smooth)
+    )(observed, beams, smooth)
 
 
 def local(observed, source_beams, source_order, initial_gains, blending):
     freqs, times = lax.axis_size("freq"), lax.axis_size("tm")
     observed_block = observed[0, 0]
-    sums, beams = terms(
-        observed_block, source_beams[0, 0], source_order.reshape(1, N), initial_gains[0]
+    sums, beams, rows = terms(
+        observed_block,
+        source_beams[0, 0],
+        source_order.reshape(1, N),
+        initial_gains[0],
+        blending,
     )
     pieces = lax.all_to_all(sums, "tm", split_axis=0, concat_axis=0, tiled=True)
     totals = jnp.sum(pieces, axis=0).reshape(3, 8, LANES)
     damped = 0.5 * (totals[:2] / totals[2])
     sent = jnp.broadcast_to(damped[None], (freqs // 2, 2, 8, LANES)).reshape(freqs, 8, LANES)
     bands = lax.all_to_all(sent, "freq", split_axis=0, concat_axis=0, tiled=True)
-    first = (lax.axis_index("freq") // 2) * 2
-    rows = lax.dynamic_slice_in_dim(blending, first, 2, 0)
     mixed = jnp.sum(rows[:, :, None, None] * bands[None], axis=1)
     spread = jnp.broadcast_to(mixed[:, None], (2, times, 8, LANES)).reshape(2 * times, 8, LANES)
     groups = [
@@ -200,8 +259,7 @@
     smooth = lax.all_to_all(
         spread, ("freq", "tm"), split_axis=0, concat_axis=0, tiled=True, axis_index_groups=groups
     )
-    slot = lax.axis_index("tm").reshape(1)
-    residual, gains_out = peel(slot, observed_block, beams, smooth)
+    residual, gains_out = peel(observed_block, beams, smooth)
     return (residual[None, None], gains_out[None])
 
 

time: 68.5 us -> 64.3 us (0.939)
  blocking collectives: 19.2 us -> 56.5 us
  waiting for transfers between devices: 19.5 us -> 0 us
  starting transfers between devices: 18.3 us -> 0 us
  local copies, waits for them, and re-layouts: 2 us -> 0.03 us
  Pallas kernels: 8.28 us -> 6.68 us
    all_to_all x0 -> x2, blocking collectives: none -> 37.4 us  [the longest x1 22 us: local(): lax.all_to_all(sent, 'freq', split_axis=0, concat_axis=0, tiled=True)]
    all_to_all x2 -> x0, waiting for transfers between devices: 19.5 us -> none  [the longest x1 10.3 us: local(): lax.all_to_all(spread, ('freq', 'tm'), split_axis=0, concat_axis=0, tiled...]
    all_to_all x2 -> x0, starting transfers between devices: 18.3 us -> none  [the longest x1 12.9 us: local(): lax.all_to_all(sent, 'freq', split_axis=0, concat_axis=0, tiled=True)]
    pallas_call x1, Pallas kernels: 3.26 us -> 2.26 us  [peel(): pl.pallas_call(peel_kernel, out_shape=(jax.ShapeDtypeStruct((2, S, S), BF...]
  transfers between devices with their start and end apart: 2 -> 0, of which waited for: 2 -> 0; matrix products, arithmetic and copies ran while one was open for 0% -> 0% of each run, Pallas kernels for 0% -> 0%
where the time goes in v2:
time: 64.3 us; the launch traced here: 64.1 us
  blocking collectives  56.5 us (88%)
  Pallas kernels  6.68 us (10%)
  between operations  0.69 us (1%)
    all_to_all x1, blocking collectives, local(): lax.all_to_all(sent, 'freq', split_axis=0, concat_axis=0, tiled=True)  22 us
    all_to_all x1, blocking collectives, local(): pieces = lax.all_to_all(sums, 'tm', split_axis=0, concat_axis=0, tiled=True)  19.2 us
    all_to_all x1, blocking collectives, local(): lax.all_to_all(spread, ('freq', 'tm'), split_axis=0, concat_axis=0, tiled...  15.4 us
    pallas_call x1, Pallas kernels, terms(): pl.pallas_call(terms_kernel, out_shape=(jax.ShapeDtypeStruct((16, 24, LAN...  4.42 us
    pallas_call x1, Pallas kernels, peel(): pl.pallas_call(peel_kernel, out_shape=(jax.ShapeDtypeStruct((2, S, S), BF...  2.26 us

profile of v2, /device:TPU:1, one launch (start us, length us, event | category | flops | bytes accessed | tf_op | source)
XLA Modules:
  0.0 64.1 jit_solution(7026512574484307468)
XLA Ops:
  0.6 4.4 %terms.1 = (f32[16,24,128]{2,1,0:T(8,128)S(1)}, bf16[2,256,512]{2,1,0:T(8,128)(2,1)S(1)}, f32[2,32]{1,0:T(2,128)S(1)}) custom-call(bf16[2,512,512]{2,1,0:T(8,128)(2,1)} %bitcast.14, bf16[2,256,512]{2,1,0:T(8,128)(2,1)} %bitcast.18, s32[1,256]{1,0:T(1,128)} %bitcast.20, f32[2,32,512]{2,1,0:T(8,128)} %bitcast.19, f32[32,32]{1,0:T(8,128)} %blending_hbm.1), custom_call_target="tpu_custom_call" | custom-call | flops 2000000000 | bytes 2000000 | tf_op jit(solution)/shard_map/terms/pallas_call | solution.py:142
  5.1 0.0 copy-start
  5.1 19.2 %all_to_all.15 = f32[16,24,128]{2,1,0:T(8,128)S(1)} all-to-all(f32[16,24,128]{2,1,0:T(8,128)S(1)} %get-tuple-element.9), channel_id=1, replica_groups=mesh['freq'=32,'tm'=16] {'tm'}, dimensions={0} | all-to-all | bytes 393216 | tf_op jit(solution)/shard_map/all_to_all | solution.py:248
  24.3 22.0 %all_to_all.16 = f32[32,8,128]{2,1,0:T(8,128)S(1)} all-to-all(f32[32,8,128]{2,1,0:T(8,128)S(1)} %bitcast.16), channel_id=1, replica_groups=mesh['freq'=32,'tm'=16] {'freq'}, dimensions={0} | all-to-all | bytes 262144 | tf_op jit(solution)/shard_map/all_to_all | solution.py:252
  46.3 0.1 multiply_reduce_fusion
  46.4 15.4 %all_to_all.17.smooth = f32[32,8,128]{2,1,0:T(8,128)S(1)} all-to-all(f32[32,8,128]{2,1,0:T(8,128)S(1)} %bitcast.17), channel_id=1, replica_groups={{0,1,2,3,4,5,6,7,8,9,10,11,12,13,14,15,16,17,18,19,20,21,22,23,24,25,26..., dimensions={0} | all-to-all | bytes 262144 | tf_op jit(solution)/shard_map/all_to_all | solution.py:259
  61.8 0.0 copy-done
  61.8 2.3 %peel.1 = (bf16[2,512,512]{2,1,0:T(8,128)(2,1)}, f32[2,2,512]{2,1,0:T(2,128)}) custom-call(bf16[2,512,512]{2,1,0:T(8,128)(2,1)S(1)} %bitcast.15, bf16[2,256,512]{2,1,0:T(8,128)(2,1)S(1)} %get-tuple-element.7.beams, f32[32,8,128]{2,1,0:T(8,128)S(1)} %all_to_all.17.smooth), custom_call_target="tpu_custom_call" | custom-call | flops 1000000000 | bytes 3000000 | tf_op jit(solution)/shard_map/peel/pallas_call | solution.py:218
  (5 shorter events, 0.1 us)
Async XLA Ops:
  5.1 56.8 %copy-start = (bf16[1,1,2,512,512]{4,3,2,1,0:T(8,128)(2,1)S(1)}, bf16[1,1,2,512,512]{4,3,2,1,0:T(8,128)(2,1)}, u32[]{:S(2)}) copy-start(bf16[1,1,2,512,512]{4,3,2,1,0:T(8,128)(2,1)} %param.5) | copy-start | bytes 3145732

commit v3 on v2

v3 whole, which is shorter than its diff:
```python
import jax
import jax.numpy as jnp
from jax import lax
from jax.experimental import pallas as pl
from jax.experimental.pallas import tpu as pltpu
from jax.sharding import PartitionSpec as P

S = 512
K = 32
P_SIZE = 8
N = K * P_SIZE
HALF = 128
GROUP = 16
LANES = 128
NT_DIMS = (((1,), (1,)), ((), ()))
NN_DIMS = (((1,), (0,)), ((), ()))
F32 = jnp.float32
BF16 = jnp.bfloat16


def dot(left, right, dims):
    return lax.dot_general(left, right, dims, preferred_element_type=F32)


def rotated_pair(real, imag, gains_real, gains_imag):
    return gains_real * real - gains_imag * imag, gains_real * imag + gains_imag * real


def repeat_rows(rows):
    return jnp.concatenate([rows] * P_SIZE, axis=0)


def direction_sums(values):
    total = values[:GROUP]
    for at in range(1, P_SIZE):
        total = total + values[at * GROUP : (at + 1) * GROUP]
    return total


def store_pair(wide, half, lanes, real, imag):
    base = half * 2 * HALF
    low, size = lanes
    real, imag = real.astype(BF16), imag.astype(BF16)
    wide[pl.ds(base, HALF), pl.ds(low, size)] = real
    wide[pl.ds(base + HALF, HALF), pl.ds(low, size)] = imag
    wide[pl.ds(base, HALF), pl.ds(S + low, size)] = -imag
    wide[pl.ds(base + HALF, HALF), pl.ds(S + low, size)] = real


def stacked_pair(reals, imags):
    joined, quarter = [], []
    for real, imag in zip(reals, imags):
        real, imag = real.astype(BF16), imag.astype(BF16)
        joined += [real, imag]
        quarter += [-imag, real]
    return jnp.concatenate(joined, axis=0), jnp.concatenate(quarter, axis=0)


def terms_kernel(
    observed_hbm, catalogue_hbm, order_hbm, gains_hbm, blending_hbm, sums, beams, rows_out,
    observed, catalogue, order, gains, blending, exact, wide, turned, misfit, arrived,
):
    copies = [
        pltpu.make_async_copy(source, target, arrived.at[at])
        for at, (source, target) in enumerate(
            (
                (order_hbm, order),
                (catalogue_hbm, catalogue),
                (gains_hbm, gains),
                (observed_hbm, observed),
                (blending_hbm, blending),
            )
        )
    ]
    for copy in copies:
        copy.start()
    copies[0].wait()
    lane = lax.broadcasted_iota(jnp.int32, (2, HALF), 1)
    listed = jnp.take_along_axis(order[...], (lane % GROUP) * P_SIZE + lane // GROUP, axis=1)
    listed = jnp.concatenate([listed[0:1], listed[1:2]], axis=1)
    source = lax.broadcasted_iota(jnp.int32, (N, N), 0)
    pick = jnp.where(source == listed, 1.0, 0.0).astype(BF16).T
    copies[1].wait()
    for part in range(2):
        picked = dot(pick, catalogue[part], NN_DIMS)
        exact[part] = picked
        beams[part] = picked.astype(BF16)
    copies[2].wait()
    copies[3].wait()
    copies[4].wait()
    rows_out[...] = blending[pl.ds((lax.axis_index("freq") // 2) * 2, 2), :]
    for half in range(2):
        rows = pl.ds(half * HALF, HALF)
        ks = pl.ds(half * GROUP, GROUP)
        real, imag = rotated_pair(
            exact[0, rows, :],
            exact[1, rows, :],
            repeat_rows(gains[0, ks, :]),
            repeat_rows(gains[1, ks, :]),
        )
        store_pair(wide, half, (0, S), real, imag)
    turned[...] = wide[:, :S].T
    for part in range(2):
        cols = pl.ds(part * S, S)
        model = dot(turned[...], wide[:, cols], NN_DIMS)
        misfit[:, cols] = (observed[part].astype(F32) - model).astype(BF16)
    everything = dot(wide[...], misfit[...], NT_DIMS)
    row_dir = lax.broadcasted_iota(jnp.int32, (HALF, HALF), 0) % GROUP
    col_dir = lax.broadcasted_iota(jnp.int32, (HALF, HALF), 1) % GROUP
    same = row_dir == col_dir
    weights = []
    for half in range(2):
        rows = pl.ds(half * HALF, HALF)
        block = wide[pl.ds(half * 2 * HALF, 2 * HALF), :S]
        grid = dot(block, block, NT_DIMS)
        gram_real = jnp.where(same, grid[:HALF, :HALF] + grid[HALF:, HALF:], 0.0)
        gram_imag = jnp.where(same, grid[:HALF, HALF:] - grid[HALF:, :HALF], 0.0)
        high_real, high_imag = gram_real.astype(BF16), gram_imag.astype(BF16)
        low_real = (gram_real - high_real.astype(F32)).astype(BF16)
        low_imag = (gram_imag - high_imag.astype(F32)).astype(BF16)
        gram = jnp.concatenate(
            [
                jnp.concatenate([high_real, high_imag, low_real, low_imag], axis=1),
                jnp.concatenate([high_imag, -high_real, low_imag, -low_real], axis=1),
            ],
            axis=0,
        )
        both = jnp.concatenate([beams[0, rows, :], beams[1, rows, :]] * 2, axis=0)
        inner = dot(gram, both, NN_DIMS)
        weights.append(
            direction_sums(exact[0, rows, :] * inner[:HALF] - exact[1, rows, :] * inner[HALF:])
        )
    for half in range(2):
        rows = pl.ds(half * HALF, HALF)
        ks = pl.ds(half * GROUP, GROUP)
        product = everything[half * 2 * HALF : (half + 1) * 2 * HALF]
        real, imag = exact[0, rows, :], exact[1, rows, :]
        weight = weights[half]
        pull_real = direction_sums(real * product[:HALF] + imag * product[HALF:])
        pull_imag = direction_sums(real * product[HALF:] - imag * product[:HALF])
        values = (
            pull_real + 2.0 * gains[0, ks, :] * weight,
            pull_imag + 2.0 * gains[1, ks, :] * weight,
            weight,
        )
        for group in range(2):
            for block in range(4):
                piece = (half * 2 + group) * 4 + block
                for part, value in enumerate(values):
                    sums[piece, pl.ds(part * 8, 8), :] = value[
                        group * 8 : group * 8 + 8, block * LANES : (block + 1) * LANES
                    ]


def terms(*operands):
    bands = operands[4].shape[0]
    return pl.pallas_call(
        terms_kernel,
        out_shape=(
            jax.ShapeDtypeStruct((16, 24, LANES), F32),
            jax.ShapeDtypeStruct((2, N, S), BF16),
            jax.ShapeDtypeStruct((2, bands), F32),
        ),
        in_specs=[pl.BlockSpec(memory_space=pltpu.HBM)] * 5,
        out_specs=(pl.BlockSpec(memory_space=pltpu.VMEM),) * 3,
        scratch_shapes=[
            pltpu.VMEM((2, S, S), BF16),
            pltpu.VMEM((2, N, S), BF16),
            pltpu.VMEM((2, HALF), jnp.int32),
            pltpu.VMEM((2, K, S), F32),
            pltpu.VMEM((bands, bands), F32),
            pltpu.VMEM((2, N, S), F32),
            pltpu.VMEM((2 * N, 2 * S), BF16),
            pltpu.VMEM((S, 2 * N), BF16),
            pltpu.VMEM((S, 2 * S), BF16),
            pltpu.SemaphoreType.DMA((5,)),
        ],
        compiler_params=pltpu.CompilerParams(vmem_limit_bytes=20 * 2**20),
        cost_estimate=pl.CostEstimate(flops=2 * 10**9, bytes_accessed=2 * 10**6, transcendentals=0),
        name="terms",
    )(*[pltpu.with_memory_space_constraint(operand, pltpu.HBM) for operand in operands])


def peel_kernel(observed, beams, smooth, residual_hbm, gains_out, residual, sent):
    pairs = []
    for half in range(2):
        rows = pl.ds(half * HALF, HALF)
        gains = [
            repeat_rows(
                jnp.concatenate(
                    [
                        jnp.concatenate(
                            [smooth[part * 16 + (2 * half + group) * 4 + block] for block in range(4)],
                            axis=1,
                        )
                        for group in range(2)
                    ],
                    axis=0,
                )
            )
            for part in range(2)
        ]
        pairs.append(
            rotated_pair(beams[0, rows, :].astype(F32), beams[1, rows, :].astype(F32), *gains)
        )
    joined, quarter = stacked_pair(*zip(*pairs))
    turned = joined.T
    copies = []
    for part, right in enumerate((joined, quarter)):
        for chunk in range(2):
            cols = pl.ds(chunk * 256, 256)
            model = dot(turned[chunk * 256 : (chunk + 1) * 256], right, NN_DIMS)
            residual[part, cols, :] = (observed[part, cols, :].astype(F32) - model).astype(BF16)
            copies.append(
                pltpu.make_async_copy(
                    residual.at[part, cols],
                    residual_hbm.at[part, cols],
                    sent.at[2 * chunk + part],
                )
            )
            copies[-1].start()
    slot = lax.axis_index("tm")
    group = slot // 4
    row = (slot % 4) * 2
    for part in range(2):
        for block in range(4):
            gains_out[part, :, pl.ds(block * LANES, LANES)] = smooth[
                part * 16 + group * 4 + block, pl.ds(row, 2), :
            ]
    for copy in copies:
        copy.wait()


def peel(observed, beams, smooth):
    vmem = pl.BlockSpec(memory_space=pltpu.VMEM)
    return pl.pallas_call(
        peel_kernel,
        out_shape=(
            jax.ShapeDtypeStruct((2, S, S), BF16),
            jax.ShapeDtypeStruct((2, 2, S), F32),
        ),
        in_specs=[vmem, vmem, vmem],
        out_specs=(pl.BlockSpec(memory_space=pltpu.HBM), vmem),
        scratch_shapes=[
            pltpu.VMEM((2, S, S), BF16),
            pltpu.SemaphoreType.DMA((4,)),
        ],
        compiler_params=pltpu.CompilerParams(vmem_limit_bytes=20 * 2**20),
        cost_estimate=pl.CostEstimate(flops=10**9, bytes_accessed=3 * 10**6, transcendentals=0),
        name="peel",
    )(observed, beams, smooth)


def local(observed, source_beams, source_order, initial_gains, blending):
    freqs, times = lax.axis_size("freq"), lax.axis_size("tm")
    observed_block = observed[0, 0]
    sums, beams, rows = terms(
        observed_block,
        source_beams[0, 0],
        source_order.reshape(2, HALF),
        initial_gains[0],
        blending,
    )
    pieces = lax.all_to_all(sums, "tm", split_axis=0, concat_axis=0, tiled=True)
    totals = jnp.sum(pieces, axis=0).reshape(3, 8, LANES)
    damped = 0.5 * (totals[:2] / totals[2])
    sent = jnp.broadcast_to(damped[None], (freqs // 2, 2, 8, LANES)).reshape(freqs, 8, LANES)
    bands = lax.all_to_all(sent, "freq", split_axis=0, concat_axis=0, tiled=True)
    mixed = jnp.sum(rows[:, :, None, None] * bands[None], axis=1)
    spread = jnp.broadcast_to(mixed[:, None], (2, times, 8, LANES)).reshape(2 * times, 8, LANES)
    groups = [
        [(pair * 2 + core) * times + time for core in range(2) for time in range(times)]
        for pair in range(freqs // 2)
    ]
    smooth = lax.all_to_all(
        spread, ("freq", "tm"), split_axis=0, concat_axis=0, tiled=True, axis_index_groups=groups
    )
    residual, gains_out = peel(observed_block, beams, smooth)
    return (residual[None, None], gains_out[None])


def solution(mesh):
    return jax.shard_map(
        local,
        mesh=mesh,
        in_specs=(
            P("freq", "tm", None, None, None),
            P("freq", "tm", None, None, None),
            P(),
            P("freq", None, None, None),
            P(),
        ),
        out_specs=(P("freq", "tm", None, None, None), P("freq", None, "tm", None)),
        check_vma=False,
    )
```

time: 64.3 us -> 63.4 us (0.986)
  Pallas kernels: 6.68 us -> 5.8 us
    pallas_call x1, Pallas kernels: 4.42 us -> 3.63 us  [terms(): pl.pallas_call(terms_kernel, out_shape=(jax.ShapeDtypeStruct((16, 24, LAN...]
where the time goes in v3:
time: 63.4 us; the launch traced here: 63.2 us
  blocking collectives  56.5 us (89%)
  Pallas kernels  5.8 us (9%)
  between operations  0.69 us (1%)
    all_to_all x1, blocking collectives, local(): lax.all_to_all(sent, 'freq', split_axis=0, concat_axis=0, tiled=True)  22 us
    all_to_all x1, blocking collectives, local(): pieces = lax.all_to_all(sums, 'tm', split_axis=0, concat_axis=0, tiled=True)  19.2 us
    all_to_all x1, blocking collectives, local(): lax.all_to_all(spread, ('freq', 'tm'), split_axis=0, concat_axis=0, tiled...  15.4 us
    pallas_call x1, Pallas kernels, terms(): pl.pallas_call(terms_kernel, out_shape=(jax.ShapeDtypeStruct((16, 24, LAN...  3.63 us
    pallas_call x1, Pallas kernels, peel(): pl.pallas_call(peel_kernel, out_shape=(jax.ShapeDtypeStruct((2, S, S), BF...  2.17 us

profile of v3, /device:TPU:1, one launch (start us, length us, event | category | flops | bytes accessed | tf_op | source)
XLA Modules:
  0.0 63.2 jit_solution(8442528491249128182)
XLA Ops:
  0.6 3.6 %terms.1 = (f32[16,24,128]{2,1,0:T(8,128)S(1)}, bf16[2,256,512]{2,1,0:T(8,128)(2,1)S(1)}, f32[2,32]{1,0:T(2,128)S(1)}) custom-call(bf16[2,512,512]{2,1,0:T(8,128)(2,1)} %bitcast.14, bf16[2,256,512]{2,1,0:T(8,128)(2,1)} %bitcast.18, s32[2,128]{1,0:T(2,128)} %bitcast.20, f32[2,32,512]{2,1,0:T(8,128)} %bitcast.19, f32[32,32]{1,0:T(8,128)} %blending_hbm.1), custom_call_target="tpu_custom_call" | custom-call | flops 2000000000 | bytes 2000000 | tf_op jit(solution)/shard_map/terms/pallas_call | solution.py:157
  4.3 0.0 copy-start
  4.3 19.2 %all_to_all.15 = f32[16,24,128]{2,1,0:T(8,128)S(1)} all-to-all(f32[16,24,128]{2,1,0:T(8,128)S(1)} %get-tuple-element.9), channel_id=1, replica_groups=mesh['freq'=32,'tm'=16] {'tm'}, dimensions={0} | all-to-all | bytes 393216 | tf_op jit(solution)/shard_map/all_to_all | solution.py:264
  23.5 22.0 %all_to_all.16 = f32[32,8,128]{2,1,0:T(8,128)S(1)} all-to-all(f32[32,8,128]{2,1,0:T(8,128)S(1)} %bitcast.16), channel_id=1, replica_groups=mesh['freq'=32,'tm'=16] {'freq'}, dimensions={0} | all-to-all | bytes 262144 | tf_op jit(solution)/shard_map/all_to_all | solution.py:268
  45.5 0.1 multiply_reduce_fusion
  45.6 15.4 %all_to_all.17.smooth = f32[32,8,128]{2,1,0:T(8,128)S(1)} all-to-all(f32[32,8,128]{2,1,0:T(8,128)S(1)} %bitcast.17), channel_id=1, replica_groups={{0,1,2,3,4,5,6,7,8,9,10,11,12,13,14,15,16,17,18,19,20,21,22,23,24,25,26..., dimensions={0} | all-to-all | bytes 262144 | tf_op jit(solution)/shard_map/all_to_all | solution.py:275
  61.0 0.0 copy-done
  61.0 2.2 %peel.1 = (bf16[2,512,512]{2,1,0:T(8,128)(2,1)}, f32[2,2,512]{2,1,0:T(2,128)}) custom-call(bf16[2,512,512]{2,1,0:T(8,128)(2,1)S(1)} %bitcast.15, bf16[2,256,512]{2,1,0:T(8,128)(2,1)S(1)} %get-tuple-element.7.beams, f32[32,8,128]{2,1,0:T(8,128)S(1)} %all_to_all.17.smooth), custom_call_target="tpu_custom_call" | custom-call | flops 1000000000 | bytes 3000000 | tf_op jit(solution)/shard_map/peel/pallas_call | solution.py:236
  (5 shorter events, 0.1 us)
Async XLA Ops:
  4.3 56.8 %copy-start = (bf16[1,1,2,512,512]{4,3,2,1,0:T(8,128)(2,1)S(1)}, bf16[1,1,2,512,512]{4,3,2,1,0:T(8,128)(2,1)}, u32[]{:S(2)}) copy-start(bf16[1,1,2,512,512]{4,3,2,1,0:T(8,128)(2,1)} %param.5) | copy-start | bytes 3145732

commit v4 on v3

--- a/solution.py
+++ b/solution.py
@@ -12,6 +12,8 @@
 HALF = 128
 GROUP = 16
 LANES = 128
+TEAM = 4
+QUARTER = 4
 NT_DIMS = (((1,), (1,)), ((), ()))
 NN_DIMS = (((1,), (0,)), ((), ()))
 F32 = jnp.float32
@@ -88,7 +90,7 @@
     copies[2].wait()
     copies[3].wait()
     copies[4].wait()
-    rows_out[...] = blending[pl.ds((lax.axis_index("freq") // 2) * 2, 2), :]
+    rows_out[...] = blending[pl.ds((lax.axis_index("freq") // TEAM) * TEAM, TEAM), :]
     for half in range(2):
         rows = pl.ds(half * HALF, HALF)
         ks = pl.ds(half * GROUP, GROUP)
@@ -159,7 +161,7 @@
         out_shape=(
             jax.ShapeDtypeStruct((16, 24, LANES), F32),
             jax.ShapeDtypeStruct((2, N, S), BF16),
-            jax.ShapeDtypeStruct((2, bands), F32),
+            jax.ShapeDtypeStruct((TEAM, bands), F32),
         ),
         in_specs=[pl.BlockSpec(memory_space=pltpu.HBM)] * 5,
         out_specs=(pl.BlockSpec(memory_space=pltpu.VMEM),) * 3,
@@ -190,10 +192,14 @@
                 jnp.concatenate(
                     [
                         jnp.concatenate(
-                            [smooth[part * 16 + (2 * half + group) * 4 + block] for block in range(4)],
+                            [
+                                smooth[(part * 2 + low) * 16 + (2 * half + group) * 4 + block]
+                                for block in range(4)
+                            ],
                             axis=1,
                         )
                         for group in range(2)
+                        for low in range(2)
                     ],
                     axis=0,
                 )
@@ -221,11 +227,12 @@
             copies[-1].start()
     slot = lax.axis_index("tm")
     group = slot // 4
-    row = (slot % 4) * 2
+    low = (slot % 4) // 2
+    row = (slot % 2) * 2
     for part in range(2):
         for block in range(4):
             gains_out[part, :, pl.ds(block * LANES, LANES)] = smooth[
-                part * 16 + group * 4 + block, pl.ds(row, 2), :
+                (part * 2 + low) * 16 + group * 4 + block, pl.ds(row, 2), :
             ]
     for copy in copies:
         copy.wait()
@@ -264,16 +271,24 @@
     pieces = lax.all_to_all(sums, "tm", split_axis=0, concat_axis=0, tiled=True)
     totals = jnp.sum(pieces, axis=0).reshape(3, 8, LANES)
     damped = 0.5 * (totals[:2] / totals[2])
-    sent = jnp.broadcast_to(damped[None], (freqs // 2, 2, 8, LANES)).reshape(freqs, 8, LANES)
-    bands = lax.all_to_all(sent, "freq", split_axis=0, concat_axis=0, tiled=True)
+    quarters = damped.reshape(TEAM, QUARTER, LANES)
+    sent = jnp.broadcast_to(quarters[None], (freqs // TEAM, TEAM, QUARTER, LANES))
+    bands = lax.all_to_all(
+        sent.reshape(freqs, QUARTER, LANES), "freq", split_axis=0, concat_axis=0, tiled=True
+    )
     mixed = jnp.sum(rows[:, :, None, None] * bands[None], axis=1)
-    spread = jnp.broadcast_to(mixed[:, None], (2, times, 8, LANES)).reshape(2 * times, 8, LANES)
+    spread = jnp.broadcast_to(mixed[:, None], (TEAM, times, QUARTER, LANES))
     groups = [
-        [(pair * 2 + core) * times + time for core in range(2) for time in range(times)]
-        for pair in range(freqs // 2)
+        [(team * TEAM + member) * times + time for member in range(TEAM) for time in range(times)]
+        for team in range(freqs // TEAM)
     ]
     smooth = lax.all_to_all(
-        spread, ("freq", "tm"), split_axis=0, concat_axis=0, tiled=True, axis_index_groups=groups
+        spread.reshape(TEAM * times, QUARTER, LANES),
+        ("freq", "tm"),
+        split_axis=0,
+        concat_axis=0,
+        tiled=True,
+        axis_index_groups=groups,
     )
     residual, gains_out = peel(observed_block, beams, smooth)
     return (residual[None, None], gains_out[None])

time: 63.4 us -> 63.5 us (level)
  no operation moved by 1% of the time
where the time goes in v4:
time: 63.5 us; the launch traced here: 63.3 us
  blocking collectives  56.5 us (89%)
  Pallas kernels  5.85 us (9%)
  between operations  0.7 us (1%)
    all_to_all x1, blocking collectives, local(): lax.all_to_all(sent.reshape(freqs, QUARTER, LANES), 'freq', split_axis=0,...  21 us
    all_to_all x1, blocking collectives, local(): pieces = lax.all_to_all(sums, 'tm', split_axis=0, concat_axis=0, tiled=True)  19.2 us
    all_to_all x1, blocking collectives, local(): lax.all_to_all(spread.reshape(TEAM * times, QUARTER, LANES), ('freq', 'tm...  16.3 us
    pallas_call x1, Pallas kernels, terms(): pl.pallas_call(terms_kernel, out_shape=(jax.ShapeDtypeStruct((16, 24, LAN...  3.63 us
    pallas_call x1, Pallas kernels, peel(): pl.pallas_call(peel_kernel, out_shape=(jax.ShapeDtypeStruct((2, S, S), BF...  2.21 us

profile of v4, /device:TPU:1, one launch (start us, length us, event | category | flops | bytes accessed | tf_op | source)
XLA Modules:
  0.0 63.3 jit_solution(5471001940319125108)
XLA Ops:
  0.6 3.6 %terms.1 = (f32[16,24,128]{2,1,0:T(8,128)S(1)}, bf16[2,256,512]{2,1,0:T(8,128)(2,1)S(1)}, f32[4,32]{1,0:T(4,128)S(1)}) custom-call(bf16[2,512,512]{2,1,0:T(8,128)(2,1)} %bitcast.10, bf16[2,256,512]{2,1,0:T(8,128)(2,1)} %bitcast.16, s32[2,128]{1,0:T(2,128)} %bitcast.18, f32[2,32,512]{2,1,0:T(8,128)} %bitcast.17, f32[32,32]{1,0:T(8,128)} %blending_hbm.1), custom_call_target="tpu_custom_call" | custom-call | flops 2000000000 | bytes 2000000 | tf_op jit(solution)/shard_map/terms/pallas_call | solution.py:159
  4.3 0.0 copy-start
  4.3 19.2 %all_to_all.15 = f32[16,24,128]{2,1,0:T(8,128)S(1)} all-to-all(f32[16,24,128]{2,1,0:T(8,128)S(1)} %get-tuple-element.9), channel_id=1, replica_groups=mesh['freq'=32,'tm'=16] {'tm'}, dimensions={0} | all-to-all | bytes 393216 | tf_op jit(solution)/shard_map/all_to_all | solution.py:271
  23.5 21.0 %all_to_all.16 = f32[32,4,128]{2,1,0:T(4,128)S(1)} all-to-all(f32[32,4,128]{2,1,0:T(4,128)S(1)} %bitcast.13), channel_id=1, replica_groups=mesh['freq'=32,'tm'=16] {'freq'}, dimensions={0} | all-to-all | bytes 131072 | tf_op jit(solution)/shard_map/all_to_all | solution.py:276
  44.6 0.1 multiply_reduce_fusion
  44.7 16.3 %all_to_all.17.smooth = f32[64,4,128]{2,1,0:T(4,128)S(1)} all-to-all(f32[64,4,128]{2,1,0:T(4,128)S(1)} %bitcast.12), channel_id=1, replica_groups={{0,1,2,3,4,5,6,7,8,9,10,11,12,13,14,15,16,17,18,19,20,21,22,23,24,25,26..., dimensions={0} | all-to-all | bytes 262144 | tf_op jit(solution)/shard_map/all_to_all | solution.py:285
  61.0 0.0 copy-done
  61.0 2.2 %peel.1 = (bf16[2,512,512]{2,1,0:T(8,128)(2,1)}, f32[2,2,512]{2,1,0:T(2,128)}) custom-call(bf16[2,512,512]{2,1,0:T(8,128)(2,1)S(1)} %bitcast.11, bf16[2,256,512]{2,1,0:T(8,128)(2,1)S(1)} %get-tuple-element.7.beams, f32[64,4,128]{2,1,0:T(4,128)S(1)} %all_to_all.17.smooth), custom_call_target="tpu_custom_call" | custom-call | flops 1000000000 | bytes 3000000 | tf_op jit(solution)/shard_map/peel/pallas_call | solution.py:243
  (8 shorter events, 0.1 us)
Async XLA Ops:
  4.3 56.8 %copy-start = (bf16[1,1,2,512,512]{4,3,2,1,0:T(8,128)(2,1)S(1)}, bf16[1,1,2,512,512]{4,3,2,1,0:T(8,128)(2,1)}, u32[]{:S(2)}) copy-start(bf16[1,1,2,512,512]{4,3,2,1,0:T(8,128)(2,1)} %param.5) | copy-start | bytes 3145732

commit v5 on v4

--- a/solution.py
+++ b/solution.py
@@ -183,7 +183,18 @@
     )(*[pltpu.with_memory_space_constraint(operand, pltpu.HBM) for operand in operands])
 
 
-def peel_kernel(observed, beams, smooth, residual_hbm, gains_out, residual, sent):
+def peel_kernel(observed, beams, smooth, residual_hbm, gains_hbm, residual, gains_out, sent):
+    slot = lax.axis_index("tm")
+    group = slot // 4
+    low = (slot % 4) // 2
+    row = (slot % 2) * 2
+    for part in range(2):
+        for block in range(4):
+            gains_out[part, :, pl.ds(block * LANES, LANES)] = smooth[
+                (part * 2 + low) * 16 + group * 4 + block, pl.ds(row, 2), :
+            ]
+    copies = [pltpu.make_async_copy(gains_out, gains_hbm, sent.at[4])]
+    copies[0].start()
     pairs = []
     for half in range(2):
         rows = pl.ds(half * HALF, HALF)
@@ -211,7 +222,6 @@
         )
     joined, quarter = stacked_pair(*zip(*pairs))
     turned = joined.T
-    copies = []
     for part, right in enumerate((joined, quarter)):
         for chunk in range(2):
             cols = pl.ds(chunk * 256, 256)
@@ -225,15 +235,6 @@
                 )
             )
             copies[-1].start()
-    slot = lax.axis_index("tm")
-    group = slot // 4
-    low = (slot % 4) // 2
-    row = (slot % 2) * 2
-    for part in range(2):
-        for block in range(4):
-            gains_out[part, :, pl.ds(block * LANES, LANES)] = smooth[
-                (part * 2 + low) * 16 + group * 4 + block, pl.ds(row, 2), :
-            ]
     for copy in copies:
         copy.wait()
 
@@ -247,10 +248,11 @@
             jax.ShapeDtypeStruct((2, 2, S), F32),
         ),
         in_specs=[vmem, vmem, vmem],
-        out_specs=(pl.BlockSpec(memory_space=pltpu.HBM), vmem),
+        out_specs=(pl.BlockSpec(memory_space=pltpu.HBM),) * 2,
         scratch_shapes=[
             pltpu.VMEM((2, S, S), BF16),
-            pltpu.SemaphoreType.DMA((4,)),
+            pltpu.VMEM((2, 2, S), F32),
+            pltpu.SemaphoreType.DMA((5,)),
         ],
         compiler_params=pltpu.CompilerParams(vmem_limit_bytes=20 * 2**20),
         cost_estimate=pl.CostEstimate(flops=10**9, bytes_accessed=3 * 10**6, transcendentals=0),

time: 63.5 us -> 62.9 us (level)
  no operation moved by 1% of the time
where the time goes in v5:
time: 62.9 us; the launch traced here: 62.6 us
  blocking collectives  56.5 us (90%)
  Pallas kernels  5.22 us (8%)
  between operations  0.7 us (1%)
    all_to_all x1, blocking collectives, local(): lax.all_to_all(sent.reshape(freqs, QUARTER, LANES), 'freq', split_axis=0,...  21 us
    all_to_all x1, blocking collectives, local(): pieces = lax.all_to_all(sums, 'tm', split_axis=0, concat_axis=0, tiled=True)  19.2 us
    all_to_all x1, blocking collectives, local(): lax.all_to_all(spread.reshape(TEAM * times, QUARTER, LANES), ('freq', 'tm...  16.3 us
    pallas_call x1, Pallas kernels, terms(): pl.pallas_call(terms_kernel, out_shape=(jax.ShapeDtypeStruct((16, 24, LAN...  3.63 us
    pallas_call x1, Pallas kernels, peel(): pl.pallas_call(peel_kernel, out_shape=(jax.ShapeDtypeStruct((2, S, S), BF...  1.59 us

profile of v5, /device:TPU:1, one launch (start us, length us, event | category | flops | bytes accessed | tf_op | source)
XLA Modules:
  0.0 62.6 jit_solution(7874199261042019072)
XLA Ops:
  0.6 3.6 %terms.1 = (f32[16,24,128]{2,1,0:T(8,128)S(1)}, bf16[2,256,512]{2,1,0:T(8,128)(2,1)S(1)}, f32[4,32]{1,0:T(4,128)S(1)}) custom-call(bf16[2,512,512]{2,1,0:T(8,128)(2,1)} %bitcast.10, bf16[2,256,512]{2,1,0:T(8,128)(2,1)} %bitcast.16, s32[2,128]{1,0:T(2,128)} %bitcast.18, f32[2,32,512]{2,1,0:T(8,128)} %bitcast.17, f32[32,32]{1,0:T(8,128)} %blending_hbm.1), custom_call_target="tpu_custom_call" | custom-call | flops 2000000000 | bytes 2000000 | tf_op jit(solution)/shard_map/terms/pallas_call | solution.py:159
  4.3 0.0 copy-start
  4.3 19.2 %all_to_all.15 = f32[16,24,128]{2,1,0:T(8,128)S(1)} all-to-all(f32[16,24,128]{2,1,0:T(8,128)S(1)} %get-tuple-element.9), channel_id=1, replica_groups=mesh['freq'=32,'tm'=16] {'tm'}, dimensions={0} | all-to-all | bytes 393216 | tf_op jit(solution)/shard_map/all_to_all | solution.py:273
  23.5 21.0 %all_to_all.16 = f32[32,4,128]{2,1,0:T(4,128)S(1)} all-to-all(f32[32,4,128]{2,1,0:T(4,128)S(1)} %bitcast.13), channel_id=1, replica_groups=mesh['freq'=32,'tm'=16] {'freq'}, dimensions={0} | all-to-all | bytes 131072 | tf_op jit(solution)/shard_map/all_to_all | solution.py:278
  44.6 0.1 multiply_reduce_fusion
  44.7 16.3 %all_to_all.17.smooth = f32[64,4,128]{2,1,0:T(4,128)S(1)} all-to-all(f32[64,4,128]{2,1,0:T(4,128)S(1)} %bitcast.12), channel_id=1, replica_groups={{0,1,2,3,4,5,6,7,8,9,10,11,12,13,14,15,16,17,18,19,20,21,22,23,24,25,26..., dimensions={0} | all-to-all | bytes 262144 | tf_op jit(solution)/shard_map/all_to_all | solution.py:287
  61.0 0.0 copy-done
  61.0 1.6 %peel.1 = (bf16[2,512,512]{2,1,0:T(8,128)(2,1)}, f32[2,2,512]{2,1,0:T(2,128)}) custom-call(bf16[2,512,512]{2,1,0:T(8,128)(2,1)S(1)} %bitcast.11, bf16[2,256,512]{2,1,0:T(8,128)(2,1)S(1)} %get-tuple-element.7.beams, f32[64,4,128]{2,1,0:T(4,128)S(1)} %all_to_all.17.smooth), custom_call_target="tpu_custom_call" | custom-call | flops 1000000000 | bytes 3000000 | tf_op jit(solution)/shard_map/peel/pallas_call | solution.py:244
  (8 shorter events, 0.1 us)
Async XLA Ops:
  4.3 56.8 %copy-start = (bf16[1,1,2,512,512]{4,3,2,1,0:T(8,128)(2,1)S(1)}, bf16[1,1,2,512,512]{4,3,2,1,0:T(8,128)(2,1)}, u32[]{:S(2)}) copy-start(bf16[1,1,2,512,512]{4,3,2,1,0:T(8,128)(2,1)} %param.5) | copy-start | bytes 3145732

commit v6 on v5

--- a/solution.py
+++ b/solution.py
@@ -13,7 +13,6 @@
 GROUP = 16
 LANES = 128
 TEAM = 4
-QUARTER = 4
 NT_DIMS = (((1,), (1,)), ((), ()))
 NN_DIMS = (((1,), (0,)), ((), ()))
 F32 = jnp.float32
@@ -90,7 +89,9 @@
     copies[2].wait()
     copies[3].wait()
     copies[4].wait()
-    rows_out[...] = blending[pl.ds((lax.axis_index("freq") // TEAM) * TEAM, TEAM), :]
+    freq = lax.axis_index("freq")
+    first = freq - 2 * ((freq // 2) % 2)
+    rows_out[...] = jnp.concatenate([blending[pl.ds(first, 1), :], blending[pl.ds(first + 2, 1), :]], axis=0)
     for half in range(2):
         rows = pl.ds(half * HALF, HALF)
         ks = pl.ds(half * GROUP, GROUP)
@@ -161,7 +162,7 @@
         out_shape=(
             jax.ShapeDtypeStruct((16, 24, LANES), F32),
             jax.ShapeDtypeStruct((2, N, S), BF16),
-            jax.ShapeDtypeStruct((TEAM, bands), F32),
+            jax.ShapeDtypeStruct((2, bands), F32),
         ),
         in_specs=[pl.BlockSpec(memory_space=pltpu.HBM)] * 5,
         out_specs=(pl.BlockSpec(memory_space=pltpu.VMEM),) * 3,
@@ -186,12 +187,11 @@
 def peel_kernel(observed, beams, smooth, residual_hbm, gains_hbm, residual, gains_out, sent):
     slot = lax.axis_index("tm")
     group = slot // 4
-    low = (slot % 4) // 2
-    row = (slot % 2) * 2
+    row = (slot % 4) * 2
     for part in range(2):
         for block in range(4):
             gains_out[part, :, pl.ds(block * LANES, LANES)] = smooth[
-                (part * 2 + low) * 16 + group * 4 + block, pl.ds(row, 2), :
+                part * 16 + group * 4 + block, pl.ds(row, 2), :
             ]
     copies = [pltpu.make_async_copy(gains_out, gains_hbm, sent.at[4])]
     copies[0].start()
@@ -203,14 +203,10 @@
                 jnp.concatenate(
                     [
                         jnp.concatenate(
-                            [
-                                smooth[(part * 2 + low) * 16 + (2 * half + group) * 4 + block]
-                                for block in range(4)
-                            ],
+                            [smooth[part * 16 + (2 * half + group) * 4 + block] for block in range(4)],
                             axis=1,
                         )
                         for group in range(2)
-                        for low in range(2)
                     ],
                     axis=0,
                 )
@@ -273,19 +269,19 @@
     pieces = lax.all_to_all(sums, "tm", split_axis=0, concat_axis=0, tiled=True)
     totals = jnp.sum(pieces, axis=0).reshape(3, 8, LANES)
     damped = 0.5 * (totals[:2] / totals[2])
-    quarters = damped.reshape(TEAM, QUARTER, LANES)
-    sent = jnp.broadcast_to(quarters[None], (freqs // TEAM, TEAM, QUARTER, LANES))
+    sent = jnp.broadcast_to(damped[None, :, None], (freqs // TEAM, 2, 2, 8, LANES))
     bands = lax.all_to_all(
-        sent.reshape(freqs, QUARTER, LANES), "freq", split_axis=0, concat_axis=0, tiled=True
+        sent.reshape(freqs, 8, LANES), "freq", split_axis=0, concat_axis=0, tiled=True
     )
     mixed = jnp.sum(rows[:, :, None, None] * bands[None], axis=1)
-    spread = jnp.broadcast_to(mixed[:, None], (TEAM, times, QUARTER, LANES))
+    spread = jnp.broadcast_to(mixed[:, None], (2, times, 8, LANES))
     groups = [
-        [(team * TEAM + member) * times + time for member in range(TEAM) for time in range(times)]
+        [(team * TEAM + side * 2 + core) * times + time for side in range(2) for time in range(times)]
         for team in range(freqs // TEAM)
+        for core in range(2)
     ]
     smooth = lax.all_to_all(
-        spread.reshape(TEAM * times, QUARTER, LANES),
+        spread.reshape(2 * times, 8, LANES),
         ("freq", "tm"),
         split_axis=0,
         concat_axis=0,

time: 62.9 us -> 61.7 us (0.981)
  blocking collectives: 56.5 us -> 55.1 us
    all_to_all x2, blocking collectives: 37.4 us -> 36 us  [the longest x1 22 us: local(): lax.all_to_all(sent.reshape(freqs, 8, LANES), 'freq', split_axis=0, conca...]
where the time goes in v6:
time: 61.7 us; the launch traced here: 61.2 us
  blocking collectives  55.1 us (89%)
  Pallas kernels  5.21 us (8%)
  between operations  0.69 us (1%)
    all_to_all x1, blocking collectives, local(): lax.all_to_all(sent.reshape(freqs, 8, LANES), 'freq', split_axis=0, conca...  22 us
    all_to_all x1, blocking collectives, local(): pieces = lax.all_to_all(sums, 'tm', split_axis=0, concat_axis=0, tiled=True)  19.2 us
    all_to_all x1, blocking collectives, local(): lax.all_to_all(spread.reshape(2 * times, 8, LANES), ('freq', 'tm'), split...  14 us
    pallas_call x1, Pallas kernels, terms(): pl.pallas_call(terms_kernel, out_shape=(jax.ShapeDtypeStruct((16, 24, LAN...  3.62 us
    pallas_call x1, Pallas kernels, peel(): pl.pallas_call(peel_kernel, out_shape=(jax.ShapeDtypeStruct((2, S, S), BF...  1.59 us

profile of v6, /device:TPU:1, one launch (start us, length us, event | category | flops | bytes accessed | tf_op | source)
XLA Modules:
  0.0 61.2 jit_solution(3734995081710070532)
XLA Ops:
  0.6 3.6 %terms.1 = (f32[16,24,128]{2,1,0:T(8,128)S(1)}, bf16[2,256,512]{2,1,0:T(8,128)(2,1)S(1)}, f32[2,32]{1,0:T(2,128)S(1)}) custom-call(bf16[2,512,512]{2,1,0:T(8,128)(2,1)} %bitcast.14, bf16[2,256,512]{2,1,0:T(8,128)(2,1)} %bitcast.18, s32[2,128]{1,0:T(2,128)} %bitcast.20, f32[2,32,512]{2,1,0:T(8,128)} %bitcast.19, f32[32,32]{1,0:T(8,128)} %blending_hbm.1), custom_call_target="tpu_custom_call" | custom-call | flops 2000000000 | bytes 2000000 | tf_op jit(solution)/shard_map/terms/pallas_call | solution.py:160
  4.3 0.0 copy-start
  4.3 19.2 %all_to_all.15 = f32[16,24,128]{2,1,0:T(8,128)S(1)} all-to-all(f32[16,24,128]{2,1,0:T(8,128)S(1)} %get-tuple-element.9), channel_id=1, replica_groups=mesh['freq'=32,'tm'=16] {'tm'}, dimensions={0} | all-to-all | bytes 393216 | tf_op jit(solution)/shard_map/all_to_all | solution.py:269
  23.5 22.0 %all_to_all.16 = f32[32,8,128]{2,1,0:T(8,128)S(1)} all-to-all(f32[32,8,128]{2,1,0:T(8,128)S(1)} %bitcast.16), channel_id=1, replica_groups=mesh['freq'=32,'tm'=16] {'freq'}, dimensions={0} | all-to-all | bytes 262144 | tf_op jit(solution)/shard_map/all_to_all | solution.py:273
  45.5 0.1 multiply_reduce_fusion
  45.6 14.0 %all_to_all.17.smooth = f32[32,8,128]{2,1,0:T(8,128)S(1)} all-to-all(f32[32,8,128]{2,1,0:T(8,128)S(1)} %bitcast.17), channel_id=1, replica_groups={{0,1,2,3,4,5,6,7,8,9,10,11,12,13,14,15,32,33,34,35,36,37,38,39,40,41,42..., dimensions={0} | all-to-all | bytes 262144 | tf_op jit(solution)/shard_map/all_to_all | solution.py:283
  59.6 0.0 copy-done
  59.6 1.6 %peel.1 = (bf16[2,512,512]{2,1,0:T(8,128)(2,1)}, f32[2,2,512]{2,1,0:T(2,128)}) custom-call(bf16[2,512,512]{2,1,0:T(8,128)(2,1)S(1)} %bitcast.15, bf16[2,256,512]{2,1,0:T(8,128)(2,1)S(1)} %get-tuple-element.7.beams, f32[32,8,128]{2,1,0:T(8,128)S(1)} %all_to_all.17.smooth), custom_call_target="tpu_custom_call" | custom-call | flops 1000000000 | bytes 3000000 | tf_op jit(solution)/shard_map/peel/pallas_call | solution.py:240
  (5 shorter events, 0.1 us)
Async XLA Ops:
  4.3 55.4 %copy-start = (bf16[1,1,2,512,512]{4,3,2,1,0:T(8,128)(2,1)S(1)}, bf16[1,1,2,512,512]{4,3,2,1,0:T(8,128)(2,1)}, u32[]{:S(2)}) copy-start(bf16[1,1,2,512,512]{4,3,2,1,0:T(8,128)(2,1)} %param.5) | copy-start | bytes 3145732

commit v7 on v6

--- a/solution.py
+++ b/solution.py
@@ -13,6 +13,8 @@
 GROUP = 16
 LANES = 128
 TEAM = 4
+FIRST_TIME = 12
+FIRST_BAND = 28
 NT_DIMS = (((1,), (1,)), ((), ()))
 NN_DIMS = (((1,), (0,)), ((), ()))
 F32 = jnp.float32
@@ -91,7 +93,8 @@
     copies[4].wait()
     freq = lax.axis_index("freq")
     first = freq - 2 * ((freq // 2) % 2)
-    rows_out[...] = jnp.concatenate([blending[pl.ds(first, 1), :], blending[pl.ds(first + 2, 1), :]], axis=0)
+    mixing = jnp.concatenate([blending[pl.ds(first, 1), :], blending[pl.ds(first + 2, 1), :]], axis=0)
+    rows_out[...] = jnp.concatenate([mixing[:, FIRST_BAND:], mixing[:, :FIRST_BAND]], axis=1)
     for half in range(2):
         rows = pl.ds(half * HALF, HALF)
         ks = pl.ds(half * GROUP, GROUP)
@@ -148,7 +151,7 @@
         )
         for group in range(2):
             for block in range(4):
-                piece = (half * 2 + group) * 4 + block
+                piece = ((half * 2 + group) * 4 + block - FIRST_TIME) % 16
                 for part, value in enumerate(values):
                     sums[piece, pl.ds(part * 8, 8), :] = value[
                         group * 8 : group * 8 + 8, block * LANES : (block + 1) * LANES
@@ -184,6 +187,10 @@
     )(*[pltpu.with_memory_space_constraint(operand, pltpu.HBM) for operand in operands])
 
 
+def gathered(part, time):
+    return part * 16 + (time + 16 - FIRST_TIME) % 16
+
+
 def peel_kernel(observed, beams, smooth, residual_hbm, gains_hbm, residual, gains_out, sent):
     slot = lax.axis_index("tm")
     group = slot // 4
@@ -191,7 +198,7 @@
     for part in range(2):
         for block in range(4):
             gains_out[part, :, pl.ds(block * LANES, LANES)] = smooth[
-                part * 16 + group * 4 + block, pl.ds(row, 2), :
+                gathered(part, group * 4 + block), pl.ds(row, 2), :
             ]
     copies = [pltpu.make_async_copy(gains_out, gains_hbm, sent.at[4])]
     copies[0].start()
@@ -203,7 +210,7 @@
                 jnp.concatenate(
                     [
                         jnp.concatenate(
-                            [smooth[part * 16 + (2 * half + group) * 4 + block] for block in range(4)],
+                            [smooth[gathered(part, (2 * half + group) * 4 + block)] for block in range(4)],
                             axis=1,
                         )
                         for group in range(2)
@@ -266,17 +273,31 @@
         initial_gains[0],
         blending,
     )
-    pieces = lax.all_to_all(sums, "tm", split_axis=0, concat_axis=0, tiled=True)
+    order = [
+        [freq * times + (at + FIRST_TIME) % times for at in range(times)] for freq in range(freqs)
+    ]
+    pieces = lax.all_to_all(
+        sums, ("freq", "tm"), split_axis=0, concat_axis=0, tiled=True, axis_index_groups=order
+    )
     totals = jnp.sum(pieces, axis=0).reshape(3, 8, LANES)
     damped = 0.5 * (totals[:2] / totals[2])
     sent = jnp.broadcast_to(damped[None, :, None], (freqs // TEAM, 2, 2, 8, LANES))
     bands = lax.all_to_all(
-        sent.reshape(freqs, 8, LANES), "freq", split_axis=0, concat_axis=0, tiled=True
+        sent.reshape(freqs, 8, LANES),
+        "freq",
+        split_axis=0,
+        concat_axis=0,
+        tiled=True,
+        axis_index_groups=[[(at + FIRST_BAND) % freqs for at in range(freqs)]],
     )
     mixed = jnp.sum(rows[:, :, None, None] * bands[None], axis=1)
     spread = jnp.broadcast_to(mixed[:, None], (2, times, 8, LANES))
     groups = [
-        [(team * TEAM + side * 2 + core) * times + time for side in range(2) for time in range(times)]
+        [
+            (team * TEAM + side * 2 + core) * times + (at + FIRST_TIME) % times
+            for side in range(2)
+            for at in range(times)
+        ]
         for team in range(freqs // TEAM)
         for core in range(2)
     ]

time: 61.7 us -> 55.5 us (0.90)
  blocking collectives: 55.1 us -> 49.2 us
    all_to_all x1, blocking collectives: 19.2 us -> 15.2 us  [local(): lax.all_to_all(sums, ('freq', 'tm'), split_axis=0, concat_axis=0, tiled=T...]
    all_to_all x1, blocking collectives: 22 us -> 20.5 us  [local(): lax.all_to_all(sent.reshape(freqs, 8, LANES), 'freq', split_axis=0, conca...]
where the time goes in v7:
time: 55.5 us; the launch traced here: 55.3 us
  blocking collectives  49.2 us (89%)
  Pallas kernels  5.23 us (9%)
  between operations  0.69 us (1%)
    all_to_all x1, blocking collectives, local(): lax.all_to_all(sent.reshape(freqs, 8, LANES), 'freq', split_axis=0, conca...  20.5 us
    all_to_all x1, blocking collectives, local(): lax.all_to_all(sums, ('freq', 'tm'), split_axis=0, concat_axis=0, tiled=T...  15.2 us
    all_to_all x1, blocking collectives, local(): lax.all_to_all(spread.reshape(2 * times, 8, LANES), ('freq', 'tm'), split...  13.4 us
    pallas_call x1, Pallas kernels, terms(): pl.pallas_call(terms_kernel, out_shape=(jax.ShapeDtypeStruct((16, 24, LAN...  3.65 us
    pallas_call x1, Pallas kernels, peel(): pl.pallas_call(peel_kernel, out_shape=(jax.ShapeDtypeStruct((2, S, S), BF...  1.57 us

profile of v7, /device:TPU:1, one launch (start us, length us, event | category | flops | bytes accessed | tf_op | source)
XLA Modules:
  0.0 55.3 jit_solution(12565868084358264266)
XLA Ops:
  0.6 3.7 %terms.1 = (f32[16,24,128]{2,1,0:T(8,128)S(1)}, bf16[2,256,512]{2,1,0:T(8,128)(2,1)S(1)}, f32[2,32]{1,0:T(2,128)S(1)}) custom-call(bf16[2,512,512]{2,1,0:T(8,128)(2,1)} %bitcast.14, bf16[2,256,512]{2,1,0:T(8,128)(2,1)} %bitcast.18, s32[2,128]{1,0:T(2,128)} %bitcast.20, f32[2,32,512]{2,1,0:T(8,128)} %bitcast.19, f32[32,32]{1,0:T(8,128)} %blending_hbm.1), custom_call_target="tpu_custom_call" | custom-call | flops 2000000000 | bytes 2000000 | tf_op jit(solution)/shard_map/terms/pallas_call | solution.py:163
  4.3 0.0 copy-start
  4.3 15.2 %all_to_all.15 = f32[16,24,128]{2,1,0:T(8,128)S(1)} all-to-all(f32[16,24,128]{2,1,0:T(8,128)S(1)} %get-tuple-element.9), channel_id=1, replica_groups={{12,13,14,15,0,1,2,3,4,5,6,7,8,9,10,11},{28,29,30,31,16,17,18,19,20,21,..., dimensions={0} | all-to-all | bytes 393216 | tf_op jit(solution)/shard_map/all_to_all | solution.py:279
  19.6 20.5 %all_to_all.16 = f32[32,8,128]{2,1,0:T(8,128)S(1)} all-to-all(f32[32,8,128]{2,1,0:T(8,128)S(1)} %bitcast.16), channel_id=1, replica_groups={{448,464,480,496,0,16,32,48,64,80,96,112,128,144,160,176,192,208,224,24..., dimensions={0} | all-to-all | bytes 262144 | tf_op jit(solution)/shard_map/all_to_all | solution.py:285
  40.1 0.1 multiply_reduce_fusion
  40.3 13.4 %all_to_all.17.smooth = f32[32,8,128]{2,1,0:T(8,128)S(1)} all-to-all(f32[32,8,128]{2,1,0:T(8,128)S(1)} %bitcast.17), channel_id=1, replica_groups={{12,13,14,15,0,1,2,3,4,5,6,7,8,9,10,11,44,45,46,47,32,33,34,35,36,37,38..., dimensions={0} | all-to-all | bytes 262144 | tf_op jit(solution)/shard_map/all_to_all | solution.py:304
  53.7 0.0 copy-done
  53.7 1.6 %peel.1 = (bf16[2,512,512]{2,1,0:T(8,128)(2,1)}, f32[2,2,512]{2,1,0:T(2,128)}) custom-call(bf16[2,512,512]{2,1,0:T(8,128)(2,1)S(1)} %bitcast.15, bf16[2,256,512]{2,1,0:T(8,128)(2,1)S(1)} %get-tuple-element.7.beams, f32[32,8,128]{2,1,0:T(8,128)S(1)} %all_to_all.17.smooth), custom_call_target="tpu_custom_call" | custom-call | flops 1000000000 | bytes 3000000 | tf_op jit(solution)/shard_map/peel/pallas_call | solution.py:247
  (5 shorter events, 0.1 us)
Async XLA Ops:
  4.3 49.4 %copy-start = (bf16[1,1,2,512,512]{4,3,2,1,0:T(8,128)(2,1)S(1)}, bf16[1,1,2,512,512]{4,3,2,1,0:T(8,128)(2,1)}, u32[]{:S(2)}) copy-start(bf16[1,1,2,512,512]{4,3,2,1,0:T(8,128)(2,1)} %param.5) | copy-start | bytes 3145732
